TPU v7x, 32 devices: a whole 2x2x4 slice. The times are simulated.
32 devices in a mesh: tens: 2 (over y), atom: 16 (over z, x, core).
Axes of the slice: x: 2, y: 2, z: 4, core: 2. Of those that a mesh axis runs over, the one named last changes fastest.
Arguments:
- chibar: float32 [96, 4096], P(None, 'atom'), may hold values from -6 to 6
- t_blocks: float32 [384, 196608], P(None, ('tens', 'atom')), may hold values from -0.3125 to 0.3125
- n_saved: float32 [96, 196608], P('tens', 'atom'), may hold values from -0.078125 to 0.078125
- q_list: int32 [2, 16, 3], P('tens', 'atom'), may hold values from 0 to 13, as said below
- q_count: int32 [2, 16], P('tens', 'atom'), may hold values from 1 to 3, as said below
Outputs:
- gbar: float32 [1024, 320], P('atom')
Inputs may be any that keep to these rules, and one draw needn't show every extreme that they name: `q_list`: the 3 entries of one pair owner's list name blocks of 3 distinct atom indices. `q_count`: equal to 3 on at least one pair owner.
All inputs are finite; a program needn't handle non-finite values.
Results may differ from a plain program's by a relative error of at most 0.0003.
Values sent between devices are 32-bit elements; how exact they have to be, the bound alone decides.
No kernel may reach another device: no remote copies, remote signals or barrier semaphores. Data moves between devices by JAX's collectives and lax.ppermute only.
A program may use at most 64 MiB of HBM per device.

v0:
```python
import jax
import jax.numpy as jnp
from jax import lax
from jax.sharding import PartitionSpec as P

BLK = 128
ORB_DEV = 64
QB_DEV = 2
REACH = 3
QL = 3


def shifted(x, axis, by):
    devices = lax.axis_size(axis)
    return lax.ppermute(x, axis, [(i, (i + by) % devices) for i in range(devices)])


def place_block(block, offset, orb_width):
    return jnp.pad(block, ((0, 0), (offset * orb_width, (2 - offset) * orb_width)))


def assemble(blocks):
    moved = []
    for by_step, row_block in ((1, 2), (-1, 0)):
        moved.append(shifted(blocks[row_block], "atom", by_step))
    return (
        place_block(moved[0], 0, ORB_DEV)
        + place_block(blocks[1], 1, ORB_DEV)
        + place_block(moved[1], 2, ORB_DEV)
    )


def local(chibar, t_blocks, n_saved, q_list, q_count):
    highest = lax.Precision.HIGHEST
    p_window = chibar.shape[0]
    band_width = 3 * ORB_DEV
    slot_ids = q_list.reshape(QL)
    in_use = q_count.reshape(())
    keeper = (jnp.arange(QL) < in_use).astype(jnp.float32)
    pieces = []
    for offset in range(-REACH, REACH + 1):
        if offset == 0:
            pieces.append(chibar)
        else:
            pieces.append(shifted(chibar, "atom", -offset))
    neighbour = jnp.concatenate(pieces, axis=1).reshape(p_window, (2 * REACH + 1) * QB_DEV, BLK)
    chosen = jnp.take(neighbour, slot_ids, axis=1)
    chosen = (chosen * keeper[None, :, None]).reshape(p_window, QL * BLK)
    mbar_local = jnp.dot(chosen, t_blocks, precision=highest, preferred_element_type=jnp.float32)
    regrouped = lax.all_to_all(mbar_local, "tens", split_axis=0, concat_axis=1, tiled=True)
    p_rows = regrouped.shape[0]
    partial_value = jnp.einsum(
        "pnm,pml->nl",
        regrouped.reshape(p_rows, band_width, ORB_DEV),
        n_saved.reshape(p_rows, ORB_DEV, band_width),
        precision=highest,
    )
    result = lax.psum(assemble(partial_value.reshape(3, ORB_DEV, band_width)), "tens")
    return result


def solution(mesh):
    placed = (
        P(None, "atom"),
        P(None, ("tens", "atom")),
        P("tens", "atom"),
        P("tens", "atom", None),
        P("tens", "atom"),
    )
    return jax.shard_map(
        local, mesh=mesh, in_specs=placed, out_specs=P("atom", None), check_vma=False
    )
```

profile of v0, /device:TPU:0, one launch (start us, length us, event | category | flops | bytes accessed | tf_op | source)
XLA Modules:
  0.0 120.9 jit_solution(3969552200305108274)
XLA Ops:
  6.5 6.0 %collective-permute-start.4 = (f32[96,256]{1,0:T(8,128)}, f32[96,256]{1,0:T(8,128)S(1)}, u32[]{:S(2)}, u32[]{:S(2)}) collective-permute-start(f32[96,256]{1,0:T(8,128)} %param.5), channel_id=1, source_target_pairs={{0,14},{1,15},{2,0},{3,1},{4,2},{5,3},{6,4},{7,5},{8,6},{9,7},{10,... | collective-permute-start | bytes 294920 | tf_op jit(solution)/shard_map/ppermute | solution.py:15
  12.5 0.0 collective-permute-start.3
  12.5 0.5 collective-permute-start.2
  13.1 0.7 collective-permute-start.1
  13.7 0.0 collective-permute-start
  13.7 0.7 fusion.7
  14.4 0.7 compare_and_fusion
  15.7 0.1 broadcast_bitcast_fusion.1
  15.8 0.1 broadcast_bitcast_fusion
  15.9 3.9 %collective-permute-done = f32[96,256]{1,0:T(8,128)S(1)} collective-permute-done((f32[96,256]{1,0:T(8,128)}, f32[96,256]{1,0:T(8,128)S(1)}, u32[]{:S(2)}, u32[]{:S(2)}) %collective-permute-start) | collective-permute-done | bytes 98336 | tf_op jit(solution)/shard_map/ppermute | solution.py:15
  19.8 2.7 %collective-permute-start.5 = (f32[96,256]{1,0:T(8,128)}, f32[96,256]{1,0:T(8,128)S(1)}, u32[]{:S(2)}, u32[]{:S(2)}) collective-permute-start(f32[96,256]{1,0:T(8,128)} %param.5), channel_id=1, source_target_pairs={{0,13},{1,14},{2,15},{3,0},{4,1},{5,2},{6,3},{7,4},{8,5},{9,6},{10... | collective-permute-start | bytes 294920 | tf_op jit(solution)/shard_map/ppermute | solution.py:15
  22.5 0.0 collective-permute-done.1
  22.5 0.0 collective-permute-done.2
  22.6 0.9 constant_dynamic-update-slice_fusion.3
  23.5 0.0 collective-permute-done.3
  23.5 0.0 collective-permute-done.4
  23.5 2.0 %collective-permute-done.5 = f32[96,256]{1,0:T(8,128)S(1)} collective-permute-done((f32[96,256]{1,0:T(8,128)}, f32[96,256]{1,0:T(8,128)S(1)}, u32[]{:S(2)}, u32[]{:S(2)}) %collective-permute-start.5) | collective-permute-done | bytes 98336 | tf_op jit(solution)/shard_map/ppermute | solution.py:15
  25.6 0.1 copy_bitcast_fusion
  25.6 0.6 gather_fusion
  26.2 0.1 copy.7
  26.3 0.1 gather.7
  26.4 9.1 %fusion = f32[2,48,6144]{2,1,0:T(8,128)} fusion(f32[384,6144]{1,0:T(8,128)} %param.6, f32[2,48,384]{2,1,0:T(8,128)S(1)} %gather.7, f32[384]{0:T(512)S(1)} %broadcast_bitcast_fusion, pred[384]{0:T(512)(128)(4,1)S(1)} %broadcast_bitcast_fusion.1), kind=kOutput, calls=%fused_computation.1 | convolution fusion | flops 2717982720 | bytes 11945856 | tf_op jit(solution)/shard_map/dot_general | solution.py:49
  35.5 4.9 %all-to-all-start = ((f32[2,48,6144]{2,1,0:T(8,128)}), f32[2,48,6144]{2,1,0:T(8,128)}, u32[]{:S(2)}, u32[]{:S(2)}) async-start(f32[2,48,6144]{2,1,0:T(8,128)} %fusion), calls=%async_computation | async-start | bytes 4718592 | tf_op jit(solution)/shard_map/all_to_all | solution.py:50
  40.4 0.0 all-reduce.5.cloned.1.call-start
  40.5 2.7 %reshape.88 = f32[48,64,192]{2,1,0:T(8,128)S(1)} reshape(f32[48,12288]{1,0:T(8,128)} %param.7) | data formatting | bytes 4718592 | tf_op jit(solution)/shard_map/reshape | solution.py:55
  43.2 24.1 %all-to-all-done = f32[2,48,6144]{2,1,0:T(8,128)} async-done(((f32[2,48,6144]{2,1,0:T(8,128)}), f32[2,48,6144]{2,1,0:T(8,128)}, u32[]{:S(2)}, u32[]{:S(2)}) %all-to-all-start) | async-done | bytes 2359328 | tf_op jit(solution)/shard_map/all_to_all | solution.py:50
  67.3 4.9 %copy.8 = f32[48,2,6144]{2,1,0:T(2,128)} copy(f32[48,2,6144]{2,0,1:T(8,128)} %bitcast.8) | data formatting | bytes 4718592 | tf_op jit(solution)/shard_map/all_to_all | solution.py:50
  72.2 5.5 %reshape.87 = f32[48,192,64]{2,1,0:T(8,128)} reshape(f32[48,2,6144]{2,1,0:T(2,128)} %copy.8) | data formatting | bytes 4718592 | tf_op jit(solution)/shard_map/reshape | solution.py:54
  77.8 5.9 %convolution_bitcast_fusion = f32[192,192]{1,0:T(8,128)S(1)} fusion(f32[48,192,64]{2,1,0:T(8,128)} %reshape.87, f32[48,64,192]{2,1,0:T(8,128)S(1)} %reshape.88), kind=kOutput, calls=%fused_computation.3 | convolution fusion | flops 1358954496 | bytes 4866048 | tf_op jit(solution)/shard_map/pnm,pml->nl/dot_general | solution.py:52
  83.7 2.1 %collective-permute-start.6 = (f32[64,192]{1,0:T(8,128)S(1)}, f32[64,192]{1,0:T(8,128)S(1)}, u32[]{:S(2)}, u32[]{:S(2)}) collective-permute-start(f32[64,192]{1,0:T(8,128)S(1)} %get-tuple-element.5), channel_id=1, source_target_pairs={{0,1},{1,2},{2,3},{3,4},{4,5},{5,6},{6,7},{7,8},{8,9},{9,10},{10,1... | collective-permute-start | bytes 147464 | tf_op jit(solution)/shard_map/ppermute | solution.py:15
  85.9 2.4 %collective-permute-start.7 = (f32[64,192]{1,0:T(8,128)S(1)}, f32[64,192]{1,0:T(8,128)S(1)}, u32[]{:S(2)}, u32[]{:S(2)}) collective-permute-start(f32[64,192]{1,0:T(8,128)S(1)} %get-tuple-element.6), channel_id=1, source_target_pairs={{0,15},{1,0},{2,1},{3,2},{4,3},{5,4},{6,5},{7,6},{8,7},{9,8},{10,9... | collective-permute-start | bytes 147464 | tf_op jit(solution)/shard_map/ppermute | solution.py:15
  88.2 2.0 %collective-permute-done.6 = f32[64,192]{1,0:T(8,128)S(1)} collective-permute-done((f32[64,192]{1,0:T(8,128)S(1)}, f32[64,192]{1,0:T(8,128)S(1)}, u32[]{:S(2)}, u32[]{:S(2)}) %collective-permute-start.6) | collective-permute-done | bytes 49184 | tf_op jit(solution)/shard_map/ppermute | solution.py:15
  90.3 0.0 collective-permute-done.7
  90.3 0.7 pad_add_fusion
  91.0 0.0 all-reduce.5.cloned.1.call-update
  91.0 21.5 %all-reduce.5.cloned.1.call-done = f32[64,320]{1,0:T(8,128)} async-done(((f32[64,320]{1,0:T(8,128)}), f32[64,320]{1,0:T(8,128)}) %all-reduce.5.cloned.1.call-update) | async-done | bytes 81936 | tf_op jit(solution)/shard_map/psum | solution.py:58
  112.5 1.5 %copy.21 = f32[64,320]{1,0:T(8,128)} copy(f32[64,320]{1,0:T(8,128)} %all-reduce.5.cloned.1.call-done) | data formatting | bytes 163840
  (9 shorter events, 0.1 us)
Async XLA Ops:
  6.5 17.0 %collective-permute-start.4 = (f32[96,256]{1,0:T(8,128)}, f32[96,256]{1,0:T(8,128)S(1)}, u32[]{:S(2)}, u32[]{:S(2)}) collective-permute-start(f32[96,256]{1,0:T(8,128)} %param.5), channel_id=1, source_target_pairs={{0,14},{1,15},{2,0},{3,1},{4,2},{5,3},{6,4},{7,5},{8,6},{9,7},{10,... | collective-permute-start | bytes 294920 | tf_op jit(solution)/shard_map/ppermute | solution.py:15
  12.5 10.9 %collective-permute-start.3 = (f32[96,256]{1,0:T(8,128)}, f32[96,256]{1,0:T(8,128)S(1)}, u32[]{:S(2)}, u32[]{:S(2)}) collective-permute-start(f32[96,256]{1,0:T(8,128)} %param.5), channel_id=1, source_target_pairs={{0,15},{1,0},{2,1},{3,2},{4,3},{5,4},{6,5},{7,6},{8,7},{9,8},{10,9... | collective-permute-start | bytes 294920 | tf_op jit(solution)/shard_map/ppermute | solution.py:15
  12.5 10.0 %collective-permute-start.2 = (f32[96,256]{1,0:T(8,128)}, f32[96,256]{1,0:T(8,128)S(1)}, u32[]{:S(2)}, u32[]{:S(2)}) collective-permute-start(f32[96,256]{1,0:T(8,128)} %param.5), channel_id=1, source_target_pairs={{0,1},{1,2},{2,3},{3,4},{4,5},{5,6},{6,7},{7,8},{8,9},{9,10},{10,1... | collective-permute-start | bytes 294920 | tf_op jit(solution)/shard_map/ppermute | solution.py:15
  13.1 9.5 %collective-permute-start.1 = (f32[96,256]{1,0:T(8,128)}, f32[96,256]{1,0:T(8,128)S(1)}, u32[]{:S(2)}, u32[]{:S(2)}) collective-permute-start(f32[96,256]{1,0:T(8,128)} %param.5), channel_id=1, source_target_pairs={{0,2},{1,3},{2,4},{3,5},{4,6},{5,7},{6,8},{7,9},{8,10},{9,11},{10,... | collective-permute-start | bytes 294920 | tf_op jit(solution)/shard_map/ppermute | solution.py:15
  13.7 6.1 %collective-permute-start = (f32[96,256]{1,0:T(8,128)}, f32[96,256]{1,0:T(8,128)S(1)}, u32[]{:S(2)}, u32[]{:S(2)}) collective-permute-start(f32[96,256]{1,0:T(8,128)} %param.5), channel_id=1, source_target_pairs={{0,3},{1,4},{2,5},{3,6},{4,7},{5,8},{6,9},{7,10},{8,11},{9,12},{10... | collective-permute-start | bytes 294920 | tf_op jit(solution)/shard_map/ppermute | solution.py:15
  19.8 5.8 %collective-permute-start.5 = (f32[96,256]{1,0:T(8,128)}, f32[96,256]{1,0:T(8,128)S(1)}, u32[]{:S(2)}, u32[]{:S(2)}) collective-permute-start(f32[96,256]{1,0:T(8,128)} %param.5), channel_id=1, source_target_pairs={{0,13},{1,14},{2,15},{3,0},{4,1},{5,2},{6,3},{7,4},{8,5},{9,6},{10... | collective-permute-start | bytes 294920 | tf_op jit(solution)/shard_map/ppermute | solution.py:15
  35.5 31.8 %all-to-all-start = ((f32[2,48,6144]{2,1,0:T(8,128)}), f32[2,48,6144]{2,1,0:T(8,128)}, u32[]{:S(2)}, u32[]{:S(2)}) async-start(f32[2,48,6144]{2,1,0:T(8,128)} %fusion), calls=%async_computation | async-start | bytes 4718592 | tf_op jit(solution)/shard_map/all_to_all | solution.py:50
  40.4 72.1 %all-reduce.5.cloned.1.call-start = ((), (), s32[]{:S(2)}) async-start(), calls=%async_computation.1 | async-start | bytes 196608 | tf_op jit(solution)/shard_map/psum | solution.py:58
  83.7 6.5 %collective-permute-start.6 = (f32[64,192]{1,0:T(8,128)S(1)}, f32[64,192]{1,0:T(8,128)S(1)}, u32[]{:S(2)}, u32[]{:S(2)}) collective-permute-start(f32[64,192]{1,0:T(8,128)S(1)} %get-tuple-element.5), channel_id=1, source_target_pairs={{0,1},{1,2},{2,3},{3,4},{4,5},{5,6},{6,7},{7,8},{8,9},{9,10},{10,1... | collective-permute-start | bytes 147464 | tf_op jit(solution)/shard_map/ppermute | solution.py:15
  85.9 4.4 %collective-permute-start.7 = (f32[64,192]{1,0:T(8,128)S(1)}, f32[64,192]{1,0:T(8,128)S(1)}, u32[]{:S(2)}, u32[]{:S(2)}) collective-permute-start(f32[64,192]{1,0:T(8,128)S(1)} %get-tuple-element.6), channel_id=1, source_target_pairs={{0,15},{1,0},{2,1},{3,2},{4,3},{5,4},{6,5},{7,6},{8,7},{9,8},{10,9... | collective-permute-start | bytes 147464 | tf_op jit(solution)/shard_map/ppermute | solution.py:15
Sparse Core Ops, SparseCore 0:
  91.2 21.3 all-reduce.4
where the time goes:
time: 121 us
  waiting for transfers between devices  53.6 us (44%)
  starting transfers between devices  19.3 us (16%)
  local copies, waits for them, and re-layouts  16.6 us (14%)
  matrix products  15 us (12%)
  between operations  14.2 us (12%)
  other arithmetic  2.07 us (2%)
    all_to_all x1, waiting for transfers between devices, local(): lax.all_to_all(mbar_local, 'tens', split_axis=0, concat_axis=1, tiled=True)  24.1 us
    psum x1, waiting for transfers between devices, local(): lax.psum(assemble(partial_value.reshape(3, ORB_DEV, band_width)), 'tens')  21.5 us
    ppermute x8, starting transfers between devices, shifted(): lax.ppermute(x, axis, [(i, (i + by) % devices) for i in range(devices)])  14.4 us
    dot_general x1, matrix products, local(): jnp.dot(chosen, t_blocks, precision=highest, preferred_element_type=jnp.f...  9.12 us
    ppermute x8, waiting for transfers between devices, shifted(): lax.ppermute(x, axis, [(i, (i + by) % devices) for i in range(devices)])  8.05 us
    dot_general x1, matrix products, local(): jnp.einsum('pnm,pml->nl', regrouped.reshape(p_rows, band_width, ORB_DEV),...  5.92 us
    reshape x1, local copies, waits for them, and re-layouts, local(): regrouped.reshape(p_rows, band_width, ORB_DEV)  5.54 us
    all_to_all x1, local copies, waits for them, and re-layouts, local(): lax.all_to_all(mbar_local, 'tens', split_axis=0, concat_axis=1, tiled=True)  4.91 us
  transfers between devices with their start and end apart: 10, of which 5 were waited for; matrix products, arithmetic and copies ran while one was open for 4% of the time, Pallas kernels for 0%

commit v1 on v0

--- a/solution.py
+++ b/solution.py
@@ -55,7 +55,9 @@
         n_saved.reshape(p_rows, ORB_DEV, band_width),
         precision=highest,
     )
-    result = lax.psum(assemble(partial_value.reshape(3, ORB_DEV, band_width)), "tens")
+    result = jnp.sum(
+        lax.all_gather(assemble(partial_value.reshape(3, ORB_DEV, band_width)), "tens"), axis=0
+    )
     return result
 
 

time: 121 us -> 90.4 us (0.75)
  waiting for transfers between devices: 53.6 us -> 32.2 us
  between operations: 14.2 us -> 0.8 us
  blocking collectives: 0 us -> 5.41 us
  local copies, waits for them, and re-layouts: 16.6 us -> 15.1 us
    psum x1 -> x0, waiting for transfers between devices: 21.5 us -> none  [local(): lax.psum(assemble(partial_value.reshape(3, ORB_DEV, band_width)), 'tens')]
    all_gather x0 -> x1, blocking collectives: none -> 5.41 us  [local(): lax.all_gather(assemble(partial_value.reshape(3, ORB_DEV, band_width)), '...]
    unnamed x7 -> x6, local copies, waits for them, and re-layouts: 2.5 us -> 0.96 us
  transfers between devices with their start and end apart: 10 -> 9, of which waited for: 5 -> 4; matrix products, arithmetic and copies ran while one was open for 4% -> 6% of each run, Pallas kernels for 0% -> 0%
where the time goes in v1:
time: 90.4 us; the launch traced here: 90 us
  waiting for transfers between devices  32.2 us (36%)
  starting transfers between devices  19.3 us (21%)
  local copies, waits for them, and re-layouts  15.1 us (17%)
  matrix products  15.1 us (17%)
  blocking collectives  5.41 us (6%)
  other arithmetic  2.07 us (2%)
    all_to_all x1, waiting for transfers between devices, local(): lax.all_to_all(mbar_local, 'tens', split_axis=0, concat_axis=1, tiled=True)  24.2 us
    ppermute x8, starting transfers between devices, shifted(): lax.ppermute(x, axis, [(i, (i + by) % devices) for i in range(devices)])  14.4 us
    dot_general x1, matrix products, local(): jnp.dot(chosen, t_blocks, precision=highest, preferred_element_type=jnp.f...  9.19 us
    ppermute x8, waiting for transfers between devices, shifted(): lax.ppermute(x, axis, [(i, (i + by) % devices) for i in range(devices)])  8.05 us
    dot_general x1, matrix products, local(): jnp.einsum('pnm,pml->nl', regrouped.reshape(p_rows, band_width, ORB_DEV),...  5.92 us
    reshape x1, local copies, waits for them, and re-layouts, local(): regrouped.reshape(p_rows, band_width, ORB_DEV)  5.55 us
    all_gather x1, blocking collectives, local(): lax.all_gather(assemble(partial_value.reshape(3, ORB_DEV, band_width)), '...  5.41 us
    all_to_all x1, local copies, waits for them, and re-layouts, local(): lax.all_to_all(mbar_local, 'tens', split_axis=0, concat_axis=1, tiled=True)  4.92 us
  transfers between devices with their start and end apart: 9, of which 4 were waited for; matrix products, arithmetic and copies ran while one was open for 6% of the time, Pallas kernels for 0%

profile of v1, /device:TPU:0, one launch (start us, length us, event | category | flops | bytes accessed | tf_op | source)
XLA Modules:
  0.0 90.0 jit_solution(13542987127607456014)
XLA Ops:
  0.0 6.0 %collective-permute-start.4 = (f32[96,256]{1,0:T(8,128)}, f32[96,256]{1,0:T(8,128)S(1)}, u32[]{:S(2)}, u32[]{:S(2)}) collective-permute-start(f32[96,256]{1,0:T(8,128)} %param.5), channel_id=1, source_target_pairs={{0,14},{1,15},{2,0},{3,1},{4,2},{5,3},{6,4},{7,5},{8,6},{9,7},{10,... | collective-permute-start | bytes 294920 | tf_op jit(solution)/shard_map/ppermute | solution.py:15
  6.0 0.0 collective-permute-start.3
  6.0 0.5 collective-permute-start.2
  6.5 0.7 collective-permute-start.1
  7.2 0.0 collective-permute-start
  7.2 0.7 fusion.7
  7.9 0.7 compare_and_fusion
  9.2 0.1 broadcast_bitcast_fusion.1
  9.3 0.1 broadcast_bitcast_fusion
  9.3 3.9 %collective-permute-done = f32[96,256]{1,0:T(8,128)S(1)} collective-permute-done((f32[96,256]{1,0:T(8,128)}, f32[96,256]{1,0:T(8,128)S(1)}, u32[]{:S(2)}, u32[]{:S(2)}) %collective-permute-start) | collective-permute-done | bytes 98336 | tf_op jit(solution)/shard_map/ppermute | solution.py:15
  13.3 2.7 %collective-permute-start.5 = (f32[96,256]{1,0:T(8,128)}, f32[96,256]{1,0:T(8,128)S(1)}, u32[]{:S(2)}, u32[]{:S(2)}) collective-permute-start(f32[96,256]{1,0:T(8,128)} %param.5), channel_id=1, source_target_pairs={{0,13},{1,14},{2,15},{3,0},{4,1},{5,2},{6,3},{7,4},{8,5},{9,6},{10... | collective-permute-start | bytes 294920 | tf_op jit(solution)/shard_map/ppermute | solution.py:15
  16.0 0.0 collective-permute-done.1
  16.0 0.0 collective-permute-done.2
  16.0 0.9 %constant_dynamic-update-slice_fusion.3 = f32[96,1792]{1,0:T(8,128)S(1)} fusion(f32[96,1792]{1,0:T(8,128)S(1)} %constant_dynamic-update-slice_fusion.4, f32[96,256]{1,0:T(8,128)} %param.5), kind=kLoop, calls=%fused_computation.14 | loop fusion | bytes 196608
  16.9 0.0 collective-permute-done.3
  17.0 0.0 collective-permute-done.4
  17.0 2.0 %collective-permute-done.5 = f32[96,256]{1,0:T(8,128)S(1)} collective-permute-done((f32[96,256]{1,0:T(8,128)}, f32[96,256]{1,0:T(8,128)S(1)}, u32[]{:S(2)}, u32[]{:S(2)}) %collective-permute-start.5) | collective-permute-done | bytes 98336 | tf_op jit(solution)/shard_map/ppermute | solution.py:15
  19.0 0.1 copy_bitcast_fusion
  19.1 0.6 gather_fusion
  19.7 0.1 copy.7
  19.8 0.1 gather.7
  19.9 9.2 %fusion = f32[2,48,6144]{2,1,0:T(8,128)} fusion(f32[384,6144]{1,0:T(8,128)} %param.6, f32[2,48,384]{2,1,0:T(8,128)S(1)} %gather.7, f32[384]{0:T(512)S(1)} %broadcast_bitcast_fusion, pred[384]{0:T(512)(128)(4,1)S(1)} %broadcast_bitcast_fusion.1), kind=kOutput, calls=%fused_computation.1 | convolution fusion | flops 2717982720 | bytes 11945856 | tf_op jit(solution)/shard_map/dot_general | solution.py:49
  29.1 4.9 %all-to-all-start = ((f32[2,48,6144]{2,1,0:T(8,128)}), f32[2,48,6144]{2,1,0:T(8,128)}, u32[]{:S(2)}, u32[]{:S(2)}) async-start(f32[2,48,6144]{2,1,0:T(8,128)} %fusion), calls=%async_computation | async-start | bytes 4718592 | tf_op jit(solution)/shard_map/all_to_all | solution.py:50
  34.0 2.7 %reshape.88 = f32[48,64,192]{2,1,0:T(8,128)S(1)} reshape(f32[48,12288]{1,0:T(8,128)} %param.7) | data formatting | bytes 4718592 | tf_op jit(solution)/shard_map/reshape | solution.py:55
  36.7 24.2 %all-to-all-done = f32[2,48,6144]{2,1,0:T(8,128)} async-done(((f32[2,48,6144]{2,1,0:T(8,128)}), f32[2,48,6144]{2,1,0:T(8,128)}, u32[]{:S(2)}, u32[]{:S(2)}) %all-to-all-start) | async-done | bytes 2359328 | tf_op jit(solution)/shard_map/all_to_all | solution.py:50
  60.9 4.9 %copy.8 = f32[48,2,6144]{2,1,0:T(2,128)} copy(f32[48,2,6144]{2,0,1:T(8,128)} %bitcast.8) | data formatting | bytes 4718592 | tf_op jit(solution)/shard_map/all_to_all | solution.py:50
  65.8 5.6 %reshape.87 = f32[48,192,64]{2,1,0:T(8,128)} reshape(f32[48,2,6144]{2,1,0:T(2,128)} %copy.8) | data formatting | bytes 4718592 | tf_op jit(solution)/shard_map/reshape | solution.py:54
  71.4 5.9 %convolution_bitcast_fusion = f32[192,192]{1,0:T(8,128)S(1)} fusion(f32[48,192,64]{2,1,0:T(8,128)} %reshape.87, f32[48,64,192]{2,1,0:T(8,128)S(1)} %reshape.88), kind=kOutput, calls=%fused_computation.3 | convolution fusion | flops 1358954496 | bytes 4866048 | tf_op jit(solution)/shard_map/pnm,pml->nl/dot_general | solution.py:52
  77.3 2.1 %collective-permute-start.6 = (f32[64,192]{1,0:T(8,128)S(1)}, f32[64,192]{1,0:T(8,128)S(1)}, u32[]{:S(2)}, u32[]{:S(2)}) collective-permute-start(f32[64,192]{1,0:T(8,128)S(1)} %get-tuple-element.5), channel_id=1, source_target_pairs={{0,1},{1,2},{2,3},{3,4},{4,5},{5,6},{6,7},{7,8},{8,9},{9,10},{10,1... | collective-permute-start | bytes 147464 | tf_op jit(solution)/shard_map/ppermute | solution.py:15
  79.4 2.4 %collective-permute-start.7 = (f32[64,192]{1,0:T(8,128)S(1)}, f32[64,192]{1,0:T(8,128)S(1)}, u32[]{:S(2)}, u32[]{:S(2)}) collective-permute-start(f32[64,192]{1,0:T(8,128)S(1)} %get-tuple-element.6), channel_id=1, source_target_pairs={{0,15},{1,0},{2,1},{3,2},{4,3},{5,4},{6,5},{7,6},{8,7},{9,8},{10,9... | collective-permute-start | bytes 147464 | tf_op jit(solution)/shard_map/ppermute | solution.py:15
  81.8 2.0 %collective-permute-done.6 = f32[64,192]{1,0:T(8,128)S(1)} collective-permute-done((f32[64,192]{1,0:T(8,128)S(1)}, f32[64,192]{1,0:T(8,128)S(1)}, u32[]{:S(2)}, u32[]{:S(2)}) %collective-permute-start.6) | collective-permute-done | bytes 49184 | tf_op jit(solution)/shard_map/ppermute | solution.py:15
  83.9 0.0 collective-permute-done.7
  83.9 0.1 pad_add_fusion
  84.0 5.4 %all-gather = f32[128,320]{1,0:T(8,128)S(1)} all-gather(f32[64,320]{1,0:T(8,128)S(1)} %pad_add_fusion), channel_id=2, replica_groups=mesh['tens'=2,'atom'=16] {'tens'}, dimensions={0}, use_global_device_ids=true | all-gather | bytes 245760 | tf_op jit(solution)/shard_map/all_gather | solution.py:59
  89.4 0.7 reduce_sum.9
  (9 shorter events, 0.1 us)
Async XLA Ops:
  0.0 17.0 %collective-permute-start.4 = (f32[96,256]{1,0:T(8,128)}, f32[96,256]{1,0:T(8,128)S(1)}, u32[]{:S(2)}, u32[]{:S(2)}) collective-permute-start(f32[96,256]{1,0:T(8,128)} %param.5), channel_id=1, source_target_pairs={{0,14},{1,15},{2,0},{3,1},{4,2},{5,3},{6,4},{7,5},{8,6},{9,7},{10,... | collective-permute-start | bytes 294920 | tf_op jit(solution)/shard_map/ppermute | solution.py:15
  6.0 10.9 %collective-permute-start.3 = (f32[96,256]{1,0:T(8,128)}, f32[96,256]{1,0:T(8,128)S(1)}, u32[]{:S(2)}, u32[]{:S(2)}) collective-permute-start(f32[96,256]{1,0:T(8,128)} %param.5), channel_id=1, source_target_pairs={{0,15},{1,0},{2,1},{3,2},{4,3},{5,4},{6,5},{7,6},{8,7},{9,8},{10,9... | collective-permute-start | bytes 294920 | tf_op jit(solution)/shard_map/ppermute | solution.py:15
  6.0 10.0 %collective-permute-start.2 = (f32[96,256]{1,0:T(8,128)}, f32[96,256]{1,0:T(8,128)S(1)}, u32[]{:S(2)}, u32[]{:S(2)}) collective-permute-start(f32[96,256]{1,0:T(8,128)} %param.5), channel_id=1, source_target_pairs={{0,1},{1,2},{2,3},{3,4},{4,5},{5,6},{6,7},{7,8},{8,9},{9,10},{10,1... | collective-permute-start | bytes 294920 | tf_op jit(solution)/shard_map/ppermute | solution.py:15
  6.5 9.5 %collective-permute-start.1 = (f32[96,256]{1,0:T(8,128)}, f32[96,256]{1,0:T(8,128)S(1)}, u32[]{:S(2)}, u32[]{:S(2)}) collective-permute-start(f32[96,256]{1,0:T(8,128)} %param.5), channel_id=1, source_target_pairs={{0,2},{1,3},{2,4},{3,5},{4,6},{5,7},{6,8},{7,9},{8,10},{9,11},{10,... | collective-permute-start | bytes 294920 | tf_op jit(solution)/shard_map/ppermute | solution.py:15
  7.2 6.1 %collective-permute-start = (f32[96,256]{1,0:T(8,128)}, f32[96,256]{1,0:T(8,128)S(1)}, u32[]{:S(2)}, u32[]{:S(2)}) collective-permute-start(f32[96,256]{1,0:T(8,128)} %param.5), channel_id=1, source_target_pairs={{0,3},{1,4},{2,5},{3,6},{4,7},{5,8},{6,9},{7,10},{8,11},{9,12},{10... | collective-permute-start | bytes 294920 | tf_op jit(solution)/shard_map/ppermute | solution.py:15
  13.3 5.8 %collective-permute-start.5 = (f32[96,256]{1,0:T(8,128)}, f32[96,256]{1,0:T(8,128)S(1)}, u32[]{:S(2)}, u32[]{:S(2)}) collective-permute-start(f32[96,256]{1,0:T(8,128)} %param.5), channel_id=1, source_target_pairs={{0,13},{1,14},{2,15},{3,0},{4,1},{5,2},{6,3},{7,4},{8,5},{9,6},{10... | collective-permute-start | bytes 294920 | tf_op jit(solution)/shard_map/ppermute | solution.py:15
  29.1 31.8 %all-to-all-start = ((f32[2,48,6144]{2,1,0:T(8,128)}), f32[2,48,6144]{2,1,0:T(8,128)}, u32[]{:S(2)}, u32[]{:S(2)}) async-start(f32[2,48,6144]{2,1,0:T(8,128)} %fusion), calls=%async_computation | async-start | bytes 4718592 | tf_op jit(solution)/shard_map/all_to_all | solution.py:50
  77.3 6.5 %collective-permute-start.6 = (f32[64,192]{1,0:T(8,128)S(1)}, f32[64,192]{1,0:T(8,128)S(1)}, u32[]{:S(2)}, u32[]{:S(2)}) collective-permute-start(f32[64,192]{1,0:T(8,128)S(1)} %get-tuple-element.5), channel_id=1, source_target_pairs={{0,1},{1,2},{2,3},{3,4},{4,5},{5,6},{6,7},{7,8},{8,9},{9,10},{10,1... | collective-permute-start | bytes 147464 | tf_op jit(solution)/shard_map/ppermute | solution.py:15
  79.4 4.4 %collective-permute-start.7 = (f32[64,192]{1,0:T(8,128)S(1)}, f32[64,192]{1,0:T(8,128)S(1)}, u32[]{:S(2)}, u32[]{:S(2)}) collective-permute-start(f32[64,192]{1,0:T(8,128)S(1)} %get-tuple-element.6), channel_id=1, source_target_pairs={{0,15},{1,0},{2,1},{3,2},{4,3},{5,4},{6,5},{7,6},{8,7},{9,8},{10,9... | collective-permute-start | bytes 147464 | tf_op jit(solution)/shard_map/ppermute | solution.py:15
